TPU v7x, 32 devices: a whole 2x2x4 slice. The times are simulated.
32 devices in a mesh: groups: 1, req: 32 (over z, y, x, core).
Axes of the slice: x: 2, y: 2, z: 4, core: 2. Of those that a mesh axis runs over, the one named last changes fastest.
Arguments:
- hidden: bfloat16 [2, 512, 2880], P(None, ('groups', 'req')), may hold values from -6 to 6
- norm_gain: bfloat16 [2880], replicated, may hold values from 0.099609375 to 1.8984375
- w_gate: bfloat16 [2880, 23040], P(None, 'req'), may hold values from -0.109375 to 0.109375
- w_up: bfloat16 [2880, 23040], P(None, 'req'), may hold values from -0.109375 to 0.109375
- w_down: bfloat16 [23040, 2880], P('req'), may hold values from -0.109375 to 0.109375
- expert_ids: int32 [2, 512, 4], P(None, ('groups', 'req')), may hold values from 0 to 7, as said below
- route_weight: float32 [2, 512, 4], P(None, ('groups', 'req')), may hold values from 0.1 to 1
Outputs:
- mixed: bfloat16 [2, 512, 2880], P(None, ('groups', 'req'))
Inputs may be any that keep to these rules, and one draw needn't show every extreme that they name: `expert_ids`: each token names 4 different experts. In each micro-batch the 16 tokens of one device name any one expert at most 12 times, and every expert is named exactly 12 times by the tokens of some device.
All inputs are finite; a program needn't handle non-finite values.
Results may differ from a plain program's by a relative error of at most 0.0058.
Values may be sent and summed in bfloat16 or wider, within the bound.
A program may use at most 128 MiB of HBM per device.

v0:
```python
import functools

import jax
import jax.numpy as jnp
from jax import lax
from jax.experimental import pallas as pl
from jax.experimental.pallas import tpu as pltpu
from jax.sharding import PartitionSpec as P

HSPLIT = 4


epsilon = 1e-05
swish_scale = 1.702


def swapped(block, axis, apart):
    count = lax.axis_size(axis)
    route = []
    for low in range(count):
        high = low | 1 << apart
        if high != low and high < count:
            route += [(low, high), (high, low)]
    return lax.ppermute(block, axis, route)


def routed_local(hidden, norm_gain, w_gate, w_up, w_down, expert_ids, route_weight):
    micro_count, tokens, model_width = hidden.shape
    top_count = expert_ids.shape[2]
    devices = lax.axis_size("req")
    experts = devices // HSPLIT
    rounded = HSPLIT * (
        (3 * tokens * top_count + 2 * experts * HSPLIT - 1) // (2 * experts * HSPLIT)
    )
    capacity = min(tokens, max(HSPLIT, rounded))
    quarter = capacity // HSPLIT
    levels = HSPLIT.bit_length() - 1
    position = lax.axis_index("req")
    gain_f32 = norm_gain.astype(jnp.float32)
    results = []
    for batch_index in range(micro_count):
        residual = hidden[batch_index].astype(jnp.float32)
        normed = (
            residual
            * lax.rsqrt(jnp.mean(residual * residual, axis=-1, keepdims=True) + epsilon)
            * gain_f32
        ).astype(jnp.bfloat16)
        flat_ids = expert_ids[batch_index].reshape(-1)
        onehot = (flat_ids[:, None] == jnp.arange(experts, dtype=jnp.int32)[None, :]).astype(
            jnp.int32
        )
        slot_index = jnp.sum((jnp.cumsum(onehot, axis=0) - onehot) * onehot, axis=1)
        target = flat_ids * capacity + slot_index
        placing = (
            target[:, None] == jnp.arange(experts * capacity, dtype=jnp.int32)[None, :]
        ).reshape(tokens, top_count, experts * capacity)
        selector = jnp.any(placing, axis=1).astype(jnp.bfloat16)
        outgoing = jnp.dot(selector.T, normed, preferred_element_type=jnp.float32).astype(
            jnp.bfloat16
        )
        copies = jnp.broadcast_to(
            outgoing.reshape(experts, 1, capacity, model_width),
            (experts, HSPLIT, capacity, model_width),
        ).reshape(devices, capacity, model_width)
        received = lax.all_to_all(copies, "req", split_axis=0, concat_axis=0, tiled=True)
        count = received.shape[1]
        slot_rows = received.reshape(-1, model_width)
        gate = jnp.dot(slot_rows, w_gate, preferred_element_type=jnp.float32)
        upward = jnp.dot(slot_rows, w_up, preferred_element_type=jnp.float32)
        act = ((upward + 1.0) * gate * jax.nn.sigmoid(swish_scale * gate)).astype(jnp.bfloat16)
        source_form = jnp.dot(act, w_down, preferred_element_type=jnp.float32).reshape(
            devices, count, model_width
        )
        shard_form = source_form.reshape(devices, HSPLIT, quarter, model_width).transpose(
            1, 0, 2, 3
        )
        folded = shard_form
        for bit_index in reversed(range(levels)):
            halfway = folded.shape[0] // 2
            upper_side = position >> bit_index & 1 == 1
            kept_part = jnp.where(upper_side, folded[halfway:], folded[:halfway])
            given_part = jnp.where(upper_side, folded[:halfway], folded[halfway:])
            folded = kept_part + swapped(given_part, "req", bit_index)
        own_rows = folded[0].astype(jnp.bfloat16)
        expert_out = lax.all_to_all(
            own_rows, "req", split_axis=0, concat_axis=0, tiled=True
        ).reshape(experts * capacity, model_width)
        weigh_table = jnp.sum(
            placing.astype(jnp.float32) * route_weight[batch_index][:, :, None], axis=1
        )
        mixture = jnp.dot(
            weigh_table, expert_out.astype(jnp.float32), precision=lax.Precision.HIGHEST
        )
        results.append((residual + mixture).astype(jnp.bfloat16))
    return jnp.stack(results, axis=0)

LANES = 128
SHARES = (9, 9, 5)
LAG = 2.0
COMPUTE_SPAN = 2.5
VMEM_BYTES = 60 * 1024 * 1024


def tree_streams(bits, micro_count, width):
    first = list(range(bits - 1, -1, -1))
    orders, shares = [first], [1]
    if bits >= 4:
        second = first[:-3] + [first[-2], first[-3], first[-1]]
        third = first[-3:-1] + first[:-3] + first[-1:]
        orders, shares = [first, second, third], SHARES
    tiles = width // LANES
    streams = []
    for batch in range(micro_count):
        for number, order in enumerate(orders):
            low = tiles * sum(shares[:number]) // sum(shares)
            high = tiles * sum(shares[: number + 1]) // sum(shares)
            if high > low:
                streams.append((batch, low * LANES, high * LANES, order))
    return streams


def later_bits(mask, order):
    last = max((place for place, bit in enumerate(order) if mask >> bit & 1), default=-1)
    return order[last + 1 :]


def last_bit(mask, order):
    return [bit for bit in order if mask >> bit & 1][-1]


def plan_steps(bits, streams, micro_count, pieces):
    devices = 1 << bits
    plan = []

    def level(mask):
        return bits if mask & 1 else bin(mask).count("1")

    def place(mask, order):
        return sum(1 << index for index, bit in enumerate(order) if mask >> bit & 1)

    begin = [bits + LAG * batch + COMPUTE_SPAN * max(0, batch - 1) for batch in range(micro_count)]
    span = [LAG or 1.0] + [COMPUTE_SPAN] * (micro_count - 1)
    end = [start + length for start, length in zip(begin, span)]
    for number, (batch, low, high, order) in enumerate(streams):
        for mask in range(1, devices):
            key = (level(mask) + LAG * batch, 0, batch, place(mask, order), number)
            plan.append((key, ("forward", number, mask)))
        for mask in range(devices):
            key = (end[batch] + bits - level(mask), 2, batch, -place(mask, order), number)
            plan.append((key, ("reduce", number, mask)))
    for batch in range(micro_count):
        for index in range(2 * pieces):
            moment = begin[batch] + span[batch] * index / (2 * pieces)
            key = (moment, 1, batch, index, 0)
            plan.append((key, ("compute", batch, 1 - index // pieces, index % pieces)))
    return [step for _, step in sorted(plan)]


def tree_kernel(
    bits,
    model_width,
    packed_ref,
    hidden_ref,
    gate_hbm,
    up_hbm,
    down_hbm,
    out_ref,
    rows,
    parts,
    arrived,
    gate_w,
    up_w,
    down_w,
    act,
    weight_sems,
    own_sem,
    ag_send,
    ag_recv,
    rs_send,
    rs_recv,
):
    micro_count, tokens, width = packed_ref.shape
    devices = 1 << bits
    group = devices // 2
    me = lax.axis_index("req")
    experts = devices // HSPLIT
    expert = me // HSPLIT
    partner = [me + (1 - 2 * ((me // (1 << bit)) % 2)) * (1 << bit) for bit in range(bits)]
    streams = tree_streams(bits, micro_count, width)

    def slot(mask):
        return (mask & 1) * group + (mask >> 1)

    loads = [
        pltpu.make_async_copy(source, target, weight_sems.at[number])
        for number, (source, target) in enumerate(
            ((gate_hbm, gate_w), (up_hbm, up_w), (down_hbm, down_w))
        )
    ]
    own = pltpu.make_async_copy(packed_ref, rows.at[:, 0], own_sem)
    own.start()

    barrier = pltpu.get_barrier_semaphore()
    for bit in range(bits):
        pl.semaphore_signal(
            barrier, inc=1, device_id={"req": partner[bit]}, device_id_type=pl.DeviceIdType.MESH
        )
    pl.semaphore_wait(barrier, bits)

    def gather_copy(number, child):
        batch, low, high, order = streams[number]
        bit = last_bit(child, order)
        mask = child - (1 << bit)
        held = packed_ref.at[batch] if mask == 0 else rows.at[batch, slot(mask)]
        return pltpu.make_async_remote_copy(
            src_ref=held.at[:, low:high],
            dst_ref=rows.at[batch, slot(child), :, low:high],
            send_sem=ag_send.at[number, child],
            recv_sem=ag_recv.at[number, child],
            device_id={"req": partner[bit]},
            device_id_type=pl.DeviceIdType.MESH,
        )

    def reduce_copy(number, mask):
        batch, low, high, order = streams[number]
        return pltpu.make_async_remote_copy(
            src_ref=parts.at[batch, slot(mask), :, low:high],
            dst_ref=arrived.at[batch, slot(mask), :, low:high],
            send_sem=rs_send.at[number, mask],
            recv_sem=rs_recv.at[number, mask],
            device_id={"req": partner[last_bit(mask, order)]},
            device_id_type=pl.DeviceIdType.MESH,
        )

    lane_of = lax.broadcasted_iota(jnp.int32, (1, width - model_width), 1)
    chosen = (lane_of == expert) | (lane_of == experts + expert)
    hidden_units = gate_w.shape[0]
    ups = [(low, min(hidden_units, low + 256)) for low in range(0, hidden_units, 256)]
    downs = [(low, min(model_width, low + 512)) for low in range(0, model_width, 512)]
    across = (((1,), (1,)), ((), ()))

    def expert_piece(batch, side, piece):
        block = rows.at[batch, pl.ds(side * group, group)]
        if piece < len(ups):
            low, high = ups[piece]
            slab = block[:, :, :model_width].reshape(group * tokens, model_width)
            gate = lax.dot_general(
                slab, gate_w[low:high, :], across, preferred_element_type=jnp.float32
            )
            upward = lax.dot_general(
                slab, up_w[low:high, :], across, preferred_element_type=jnp.float32
            )
            act[:, low:high] = (
                (upward + 1.0) * gate * jax.nn.sigmoid(swish_scale * gate)
            ).astype(jnp.bfloat16)
            return
        low, high = downs[piece - len(ups)]
        tail = block[:, :, model_width:].reshape(group * tokens, width - model_width)
        weight = jnp.sum(
            jnp.where(chosen, tail.astype(jnp.float32), 0.0), axis=1, keepdims=True
        )
        part = jnp.dot(act[...], down_w[:, low:high], preferred_element_type=jnp.float32)
        parts[batch, pl.ds(side * group, group), :, low:high] = (
            (part * weight).astype(parts.dtype).reshape(group, tokens, high - low)
        )

    for batch in range(micro_count):
        for place in range(bits):
            for number, stream in enumerate(streams):
                if stream[0] == batch:
                    gather_copy(number, 1 << stream[3][place]).start()
    for load in loads:
        load.start()
    parts[:, :, :, model_width:] = jnp.zeros(
        (micro_count, devices, tokens, width - model_width), parts.dtype
    )
    own.wait()

    pieces = len(ups) + len(downs)
    loaded = False
    for step in plan_steps(bits, streams, micro_count, pieces):
        if step[0] == "forward":
            _, number, mask = step
            gather_copy(number, mask).wait_recv()
            for bit in later_bits(mask, streams[number][3]):
                gather_copy(number, mask + (1 << bit)).start()
        elif step[0] == "compute":
            if not loaded:
                loaded = True
                for load in loads:
                    load.wait()
            expert_piece(*step[1:])
        else:
            _, number, mask = step
            batch, low, high, order = streams[number]
            children = [mask + (1 << bit) for bit in later_bits(mask, order)]
            if not mask:
                high = min(high, model_width)
            if children:
                total = parts[batch, slot(mask), :, low:high].astype(jnp.float32)
                if not mask:
                    total = hidden_ref[batch, :, low:high].astype(jnp.float32) + total
                for child in reversed(children):
                    reduce_copy(number, child).wait_recv()
                    total = total + arrived[batch, slot(child), :, low:high].astype(jnp.float32)
                if mask:
                    parts[batch, slot(mask), :, low:high] = total.astype(parts.dtype)
                else:
                    out_ref[batch, :, low:high] = total.astype(out_ref.dtype)
            if mask:
                reduce_copy(number, mask).start()
    for number in range(len(streams)):
        for mask in range(1, devices):
            gather_copy(number, mask).wait_send()
            reduce_copy(number, mask).wait_send()


def tree_local(hidden, norm_gain, w_gate, w_up, w_down, expert_ids, route_weight):
    micro_count, tokens, model_width = hidden.shape
    devices = lax.axis_size("req")
    bits = devices.bit_length() - 1
    experts = devices // HSPLIT
    width = padded(model_width)
    hidden_units = w_gate.shape[1]
    residual = hidden.astype(jnp.float32)
    normed = (
        residual
        * lax.rsqrt(jnp.mean(residual * residual, axis=-1, keepdims=True) + epsilon)
        * norm_gain.astype(jnp.float32)
    ).astype(jnp.bfloat16)
    named = expert_ids[..., None] == jnp.arange(experts, dtype=jnp.int32)
    table = jnp.sum(jnp.where(named, route_weight[..., None], 0.0), axis=2)
    upper = lax.reduce_precision(table, 8, 7)
    lower = table - upper
    filler = width - model_width - 2 * experts
    packed = jnp.concatenate(
        [
            normed,
            upper.astype(jnp.bfloat16),
            lower.astype(jnp.bfloat16),
            jnp.zeros((micro_count, tokens, filler), jnp.bfloat16),
        ],
        axis=-1,
    )
    vmem = pl.BlockSpec(memory_space=pltpu.VMEM)
    hbm = pl.BlockSpec(memory_space=pl.ANY)
    slots = (micro_count, devices, tokens, width)
    streams = len(tree_streams(bits, micro_count, width))
    return pl.pallas_call(
        functools.partial(tree_kernel, bits, model_width),
        out_shape=jax.ShapeDtypeStruct(hidden.shape, hidden.dtype),
        in_specs=[vmem, vmem, hbm, hbm, hbm],
        out_specs=vmem,
        scratch_shapes=[
            pltpu.VMEM(slots, jnp.bfloat16),
            pltpu.VMEM(slots, jnp.bfloat16),
            pltpu.VMEM(slots, jnp.bfloat16),
            pltpu.VMEM((hidden_units, model_width), w_gate.dtype),
            pltpu.VMEM((hidden_units, model_width), w_up.dtype),
            pltpu.VMEM((hidden_units, model_width), w_down.dtype),
            pltpu.VMEM((devices // 2 * tokens, hidden_units), jnp.bfloat16),
            pltpu.SemaphoreType.DMA((3,)),
            pltpu.SemaphoreType.DMA,
            pltpu.SemaphoreType.DMA((streams, devices)),
            pltpu.SemaphoreType.DMA((streams, devices)),
            pltpu.SemaphoreType.DMA((streams, devices)),
            pltpu.SemaphoreType.DMA((streams, devices)),
        ],
        compiler_params=pltpu.CompilerParams(
            collective_id=0, has_side_effects=True, vmem_limit_bytes=VMEM_BYTES
        ),
        name="tree",
    )(packed, hidden, w_gate.T, w_up.T, w_down)


def padded(size):
    return -(-size // LANES) * LANES


def tree_fits(hidden, norm_gain, w_gate, w_up, w_down, expert_ids, route_weight):
    micro_count, tokens, model_width = hidden.shape
    devices = lax.axis_size("req")
    width = padded(model_width)
    units = w_gate.shape[1]
    slots = 3 * micro_count * devices * tokens * width
    weights = 3 * units * width
    work = 3 * devices * tokens * width
    return (
        devices & (devices - 1) == 0
        and 2 * (devices // HSPLIT) <= width - model_width
        and 2 * (slots + weights + work) <= VMEM_BYTES
    )


def local(*arguments):
    return (tree_local if tree_fits(*arguments) else routed_local)(*arguments)


def solution(mesh):
    return jax.shard_map(
        local,
        mesh=mesh,
        in_specs=(
            P(None, ("groups", "req"), None),
            P(),
            P(None, "req"),
            P(None, "req"),
            P("req", None),
            P(None, ("groups", "req"), None),
            P(None, ("groups", "req"), None),
        ),
        out_specs=P(None, ("groups", "req"), None),
        check_vma=False,
    )
```

profile of v0, /device:TPU:0, one launch (start us, length us, event | category | flops | bytes accessed | tf_op | source)
XLA Modules:
  0.0 85.5 jit_solution(1827802866869281687)
XLA Ops:
  0.0 1.0 %fusion = f32[2,16]{1,0:T(2,128)S(1)} fusion(bf16[2,16,2880]{2,1,0:T(8,128)(2,1)} %hidden_ref.1), kind=kLoop, calls=%fused_computation.2 | loop fusion | flops 276448 | bytes 184448 | tf_op jit(solution)/shard_map/reduce_sum | solution.py:328
  1.1 0.7 select_reduce_fusion
  1.8 0.1 copy.13
  1.9 0.1 copy.12
  1.9 0.7 convert_element_type.16
  2.6 1.0 %fusion.2 = bf16[2,16,2880]{2,1,0:T(8,128)(2,1)S(1)} fusion(bf16[2,16,2880]{2,1,0:T(8,128)(2,1)} %hidden_ref.1, f32[2880]{0:T(1024)S(1)} %convert_element_type.16, f32[2,16]{1,0:T(2,128)S(1)} %add_rsqrt_fusion), kind=kLoop, calls=%fused_computation.4 | loop fusion | flops 368640 | bytes 380288 | tf_op jit(solution)/shard_map/convert_element_type | solution.py:330
  3.7 0.8 concatenate.3.packed_ref
  4.5 79.4 %tree.1 = bf16[2,16,2880]{2,1,0:T(8,128)(2,1)} custom-call(bf16[2,16,2944]{2,1,0:T(8,128)(2,1)} %concatenate.3.packed_ref, bf16[2,16,2880]{2,1,0:T(8,128)(2,1)} %hidden_ref.1, bf16[720,2880]{1,0:T(8,128)(2,1)} %bitcast.2, bf16[720,2880]{1,0:T(8,128)(2,1)} %bitcast.3, bf16[720,2880]{1,0:T(8,128)(2,1)} %down_hbm.1), custom_call_target="tpu_custom_call" | custom-call | tf_op jit(solution)/shard_map/tree/pallas_call | solution.py:349
  83.8 1.6 %copy.16 = bf16[2,16,2880]{2,1,0:T(8,128)(2,1)} copy(bf16[2,16,2880]{2,1,0:T(8,128)(2,1)} %tree.1) | data formatting | bytes 368640
  (4 shorter events, 0.0 us)
where the time goes:
time: 85.7 us; the launch traced here: 85.5 us
  Pallas kernels  79.4 us (93%)
  other arithmetic  3.52 us (4%)
  local copies, waits for them, and re-layouts  2.53 us (3%)
    pallas_call x1, Pallas kernels, tree_local(): pl.pallas_call(functools.partial(tree_kernel, bits, model_width), out_sha...  79.4 us

commit v1 on v0

v1 whole, which is shorter than its diff:
```python
import functools

import jax
import jax.numpy as jnp
from jax import lax
from jax.experimental import pallas as pl
from jax.experimental.pallas import tpu as pltpu
from jax.sharding import PartitionSpec as P

HSPLIT = 4


epsilon = 1e-05
swish_scale = 1.702


def swapped(block, axis, apart):
    count = lax.axis_size(axis)
    route = []
    for low in range(count):
        high = low | 1 << apart
        if high != low and high < count:
            route += [(low, high), (high, low)]
    return lax.ppermute(block, axis, route)


def routed_local(hidden, norm_gain, w_gate, w_up, w_down, expert_ids, route_weight):
    micro_count, tokens, model_width = hidden.shape
    top_count = expert_ids.shape[2]
    devices = lax.axis_size("req")
    experts = devices // HSPLIT
    rounded = HSPLIT * (
        (3 * tokens * top_count + 2 * experts * HSPLIT - 1) // (2 * experts * HSPLIT)
    )
    capacity = min(tokens, max(HSPLIT, rounded))
    quarter = capacity // HSPLIT
    levels = HSPLIT.bit_length() - 1
    position = lax.axis_index("req")
    gain_f32 = norm_gain.astype(jnp.float32)
    results = []
    for batch_index in range(micro_count):
        residual = hidden[batch_index].astype(jnp.float32)
        normed = (
            residual
            * lax.rsqrt(jnp.mean(residual * residual, axis=-1, keepdims=True) + epsilon)
            * gain_f32
        ).astype(jnp.bfloat16)
        flat_ids = expert_ids[batch_index].reshape(-1)
        onehot = (flat_ids[:, None] == jnp.arange(experts, dtype=jnp.int32)[None, :]).astype(
            jnp.int32
        )
        slot_index = jnp.sum((jnp.cumsum(onehot, axis=0) - onehot) * onehot, axis=1)
        target = flat_ids * capacity + slot_index
        placing = (
            target[:, None] == jnp.arange(experts * capacity, dtype=jnp.int32)[None, :]
        ).reshape(tokens, top_count, experts * capacity)
        selector = jnp.any(placing, axis=1).astype(jnp.bfloat16)
        outgoing = jnp.dot(selector.T, normed, preferred_element_type=jnp.float32).astype(
            jnp.bfloat16
        )
        copies = jnp.broadcast_to(
            outgoing.reshape(experts, 1, capacity, model_width),
            (experts, HSPLIT, capacity, model_width),
        ).reshape(devices, capacity, model_width)
        received = lax.all_to_all(copies, "req", split_axis=0, concat_axis=0, tiled=True)
        count = received.shape[1]
        slot_rows = received.reshape(-1, model_width)
        gate = jnp.dot(slot_rows, w_gate, preferred_element_type=jnp.float32)
        upward = jnp.dot(slot_rows, w_up, preferred_element_type=jnp.float32)
        act = ((upward + 1.0) * gate * jax.nn.sigmoid(swish_scale * gate)).astype(jnp.bfloat16)
        source_form = jnp.dot(act, w_down, preferred_element_type=jnp.float32).reshape(
            devices, count, model_width
        )
        shard_form = source_form.reshape(devices, HSPLIT, quarter, model_width).transpose(
            1, 0, 2, 3
        )
        folded = shard_form
        for bit_index in reversed(range(levels)):
            halfway = folded.shape[0] // 2
            upper_side = position >> bit_index & 1 == 1
            kept_part = jnp.where(upper_side, folded[halfway:], folded[:halfway])
            given_part = jnp.where(upper_side, folded[:halfway], folded[halfway:])
            folded = kept_part + swapped(given_part, "req", bit_index)
        own_rows = folded[0].astype(jnp.bfloat16)
        expert_out = lax.all_to_all(
            own_rows, "req", split_axis=0, concat_axis=0, tiled=True
        ).reshape(experts * capacity, model_width)
        weigh_table = jnp.sum(
            placing.astype(jnp.float32) * route_weight[batch_index][:, :, None], axis=1
        )
        mixture = jnp.dot(
            weigh_table, expert_out.astype(jnp.float32), precision=lax.Precision.HIGHEST
        )
        results.append((residual + mixture).astype(jnp.bfloat16))
    return jnp.stack(results, axis=0)

LANES = 128
PLANES = 4
CORE, X, Y, Z = 1, 2, 4, 8
SHARES = ((8, "zyx"), (10, "zxy"), (5, "yxz"))
VMEM_BYTES = 60 * 1024 * 1024
LINK_RATE, CORE_RATE = 47.5e3, 350e3
CORE_DELAY, HOP_DELAY, FURTHER_DELAY = 1.0, 1.7, 0.8
UP_SPAN, DOWN_SPAN, ADD_SPAN, STEP_SPAN = 0.9, 0.5, 0.01, 0.02
ROW = slice(0, 1)
PAIR = slice(0, 2)


def padded(size):
    return -(-size // LANES) * LANES


def lane_streams(width):
    tiles, total, low, streams = width // LANES, sum(share for share, _ in SHARES), 0, []
    for number, (share, order) in enumerate(SHARES):
        taken = sum(part for part, _ in SHARES[: number + 1])
        high = tiles * taken // total * LANES
        streams.append((low, high, order))
        low = high
    return streams


def one(value):
    return slice(value, value + 1)


def block(order, first, second, depth):
    return (first, second, depth) if order == "zyx" else (second, first, depth)


def gather_messages(order):
    every, later = slice(0, PLANES), slice(1, PLANES)
    own = (ROW, ROW, ROW)
    messages = []
    if order == "yxz":
        square = (PAIR, PAIR, ROW)
        messages += [
            ("y0", Y, own, ()),
            ("x0", X, own, ()),
            ("xy", X, (ROW, one(1), ROW), ("y0",)),
            ("z2", 2 * Z, square, ("x0", "xy")),
            ("z1", Z, square, ("x0", "xy")),
            ("z3", Z, (PAIR, PAIR, one(2)), ("z2",)),
            ("c0", CORE, square, ("x0", "xy")),
            ("c2", CORE, (PAIR, PAIR, one(2)), ("z2",)),
            ("c1", CORE, (PAIR, PAIR, one(1)), ("z1",)),
            ("c3", CORE, (PAIR, PAIR, one(3)), ("z3",)),
        ]
        return messages
    far, near = (X, Y) if order == "zyx" else (Y, X)
    planes = tuple("z%d" % plane for plane in range(1, PLANES))
    messages += [("z%d" % plane, plane * Z, own, ()) for plane in range(1, PLANES)]
    messages += [
        ("n0", near, own, ()),
        ("f0", far, own, ()),
        ("nz", near, (ROW, ROW, later), planes),
        ("fz", far, (ROW, ROW, later), planes),
        ("fn", far, block(order, ROW, one(1), ROW), ("n0",)),
        ("fnz", far, block(order, ROW, one(1), later), ("nz",)),
        ("c0", CORE, own, ()),
        ("cz", CORE, (ROW, ROW, later), planes),
        ("cn", CORE, block(order, ROW, one(1), every), ("n0", "nz")),
        ("cf", CORE, block(order, one(1), ROW, every), ("f0", "fz")),
        ("cfn", CORE, block(order, one(1), one(1), every), ("fn", "fnz")),
    ]
    return messages


def reduce_steps(order):
    every, later = slice(0, PLANES), slice(1, PLANES)
    own = (ROW, ROW, ROW)
    if order == "yxz":
        at = lambda plane: (PAIR, PAIR, one(plane))
        return [
            (at(3), [("z3", Z, at(3))], []),
            (at(1), [("z1", Z, at(1))], []),
            (at(2), [("z2", 2 * Z, at(2))], [("z3", at(3))]),
            (
                (one(1), PAIR, ROW),
                [("x", X, (one(1), PAIR, ROW))],
                [("z1", (one(1), PAIR, one(1))), ("z2", (one(1), PAIR, one(2)))],
            ),
            (
                (ROW, one(1), ROW),
                [("y", Y, (ROW, one(1), ROW))],
                [
                    ("z1", (ROW, one(1), one(1))),
                    ("z2", (ROW, one(1), one(2))),
                    ("x", (one(1), one(1), ROW)),
                ],
            ),
            (
                own,
                [],
                [
                    ("z1", (ROW, ROW, one(1))),
                    ("z2", (ROW, ROW, one(2))),
                    ("x", (one(1), ROW, ROW)),
                    ("y", (ROW, one(1), ROW)),
                ],
            ),
        ]
    far, near = (X, Y) if order == "zyx" else (Y, X)
    at = functools.partial(block, order)
    corner, side, face = at(one(1), one(1), every), at(one(1), ROW, every), at(ROW, one(1), every)
    planes = [(ROW, ROW, one(plane)) for plane in range(1, PLANES)]
    names = ["z%d" % plane for plane in range(1, PLANES)]
    return [
        (corner, [("fn", far, corner)], []),
        (side, [("f", far, side)], []),
        (face, [("n", near, face)], [("fn", corner)]),
        (
            (ROW, ROW, later),
            [(name, plane * Z, planes[plane - 1]) for plane, name in enumerate(names, 1)],
            [("f", at(one(1), ROW, later)), ("n", at(ROW, one(1), later))],
        ),
        (
            own,
            [],
            [("f", at(one(1), ROW, ROW)), ("n", at(ROW, one(1), ROW))] + list(zip(names, planes)),
        ),
    ]


def rows_of(rows):
    return [
        (x, y, z)
        for x in range(rows[0].start, rows[0].stop)
        for y in range(rows[1].start, rows[1].stop)
        for z in range(rows[2].start, rows[2].stop)
    ]


def lane_pieces(low, high, size):
    return [(start, min(high, start + size)) for start in range(low, high, size)]


def all_actions(micro_count, tokens, width, model_width, ups):
    streams = lane_streams(width)
    actions = []
    for batch in range(micro_count):
        for number, (low, high, order) in enumerate(streams):
            for name, hop, rows, needs in gather_messages(order):
                label = ("g", batch, number, name)
                needed = [("g", batch, number, need) for need in needs]
                if batch and not needs:
                    needed = [("s", batch - 1, 0, "fz"), ("s", batch - 1, 1, "fz")]
                size = 2 * len(rows_of(rows)) * tokens * (high - low)
                actions.append((("s", batch, number, name), needed, STEP_SPAN, [(label, hop, size)]))
    for batch in range(micro_count):
        for number, (low, high, order) in enumerate(streams):
            for index, (rows, sends, arrived) in enumerate(reduce_steps(order)):
                needed = [("d", batch, number, 0), ("r", batch, number, "c")]
                needed += [("r", batch, number, name) for name, _ in arrived]
                count = len(rows_of(rows))
                made = [
                    (("r", batch, number, name), hop, 2 * len(rows_of(sent)) * tokens * (high - low))
                    for name, hop, sent in sends
                ]
                span = STEP_SPAN + ADD_SPAN * count * (2 + len(arrived)) * (high - low) / 1024
                actions.append((("a", batch, number, index), needed, span, made))
    for batch in range(micro_count):
        done = []
        for side in (0, 1):
            for piece in range(len(ups)):
                needed = [
                    ("g", batch, number, name)
                    for number, (_, _, order) in enumerate(streams)
                    for name, hop, _, _ in gather_messages(order)
                    if (hop == CORE) == bool(side)
                ]
                actions.append((("u", batch, side, piece), needed + done[-1:], UP_SPAN, []))
                done.append(("u", batch, side, piece))
        for number, (low, high, order) in enumerate(streams):
            for side in (1, 0):
                made = []
                if side:
                    size = 2 * PLANES * 4 * tokens * (high - low)
                    made = [(("r", batch, number, "c"), CORE, size)]
                span = DOWN_SPAN * (high - low) / 1024
                actions.append((("d", batch, number, side), done[-1:], span, made))
                done.append(("d", batch, number, side))
    return actions


def plan_actions(actions):
    moment, ready_at, link_free, order = 0.0, {}, {}, []
    left = list(actions)
    while left:
        best = None
        for action in left:
            if all(need in ready_at for need in action[1]):
                start = max([ready_at[need] for need in action[1]], default=0.0)
                if start <= moment:
                    best = (moment, action)
                    break
                if best is None or start < best[0]:
                    best = (start, action)
        start, action = best
        left.remove(action)
        order.append(action)
        moment = max(moment, start) + action[2]
        ready_at[action[0]] = moment
        for label, hop, size in action[3]:
            link = "z" if hop >= Z else hop
            rate = CORE_RATE if hop == CORE else LINK_RATE
            delay = CORE_DELAY if hop == CORE else HOP_DELAY + FURTHER_DELAY * (hop > Z)
            link_free[link] = max(link_free.get(link, 0.0), moment) + size / rate
            ready_at[label] = link_free[link] + delay
    return order, moment


def tree_kernel(
    hidden_ref,
    gain_ref,
    ids_ref,
    weight_ref,
    gate_hbm,
    up_hbm,
    down_hbm,
    out_ref,
    rows,
    parts,
    arrived,
    gate_w,
    up_w,
    down_w,
    act,
    weight_sems,
    send_sems,
    recv_sems,
):
    micro_count, tokens, model_width = hidden_ref.shape
    width = rows.shape[-1]
    devices = lax.axis_size("req")
    group = devices // 2
    me = lax.axis_index("req")
    experts = devices // HSPLIT
    expert = me // HSPLIT
    streams = lane_streams(width)
    hops = [CORE, X, Y] + [plane * Z for plane in range(1, PLANES)]

    def across(hop):
        if hop < Z:
            return me + (1 - 2 * ((me // hop) % 2)) * hop
        plane, flips = me // Z, hop // Z
        low = plane % 2 + (flips % 2) * (1 - 2 * (plane % 2))
        high = plane // 2 + (flips // 2) * (1 - 2 * (plane // 2))
        return me % Z + Z * (2 * high + low)

    partner = {hop: across(hop) for hop in hops}
    barrier = pltpu.get_barrier_semaphore()
    for hop in hops:
        pl.semaphore_signal(
            barrier, inc=1, device_id={"req": partner[hop]}, device_id_type=pl.DeviceIdType.MESH
        )
    loads = [
        pltpu.make_async_copy(source, target, weight_sems.at[number])
        for number, (source, target) in enumerate(
            ((gate_hbm, gate_w), (up_hbm, up_w), (down_hbm, down_w))
        )
    ]
    for load in loads:
        load.start()

    tail = width - model_width
    lane_of = lax.broadcasted_iota(jnp.int32, (1, tail), 1)
    gain = gain_ref[...].astype(jnp.float32)
    for batch in range(micro_count):
        residual = hidden_ref[batch].astype(jnp.float32)
        scale = lax.rsqrt(jnp.mean(residual * residual, axis=-1, keepdims=True) + epsilon)
        rows[batch, 0, 0, 0, 0, :, :model_width] = (residual * scale * gain).astype(jnp.bfloat16)
        named = lane_of - experts * (lane_of // experts)
        table = jnp.zeros((tokens, tail), jnp.float32)
        for member in range(ids_ref.shape[2]):
            table = table + jnp.where(
                ids_ref[batch, :, member : member + 1] == named,
                weight_ref[batch, :, member : member + 1],
                0.0,
            )
        upper = table.astype(jnp.bfloat16).astype(jnp.float32)
        shown = jnp.where(lane_of < experts, upper, table - upper)
        shown = jnp.where(lane_of < 2 * experts, shown, 0.0)
        rows[batch, 0, 0, 0, 0, :, model_width:] = shown.astype(jnp.bfloat16)
    pl.semaphore_wait(barrier, len(hops))

    slots = {}

    def remote(source, target, label, hop):
        number = slots.setdefault(label, len(slots))
        return pltpu.make_async_remote_copy(
            src_ref=source,
            dst_ref=target,
            send_sem=send_sems.at[number],
            recv_sem=recv_sems.at[number],
            device_id={"req": partner[hop]},
            device_id_type=pl.DeviceIdType.MESH,
        )

    copies = {}
    for batch in range(micro_count):
        for number, (low, high, order) in enumerate(streams):
            lanes = slice(low, high)
            for name, hop, (xs, ys, zs), _ in gather_messages(order):
                flip = lambda part, bit: one(part.start ^ 1) if hop == bit else part
                landing = (flip(xs, X), flip(ys, Y), zs)
                if hop >= Z:
                    landing = (xs, ys, one(zs.start ^ (hop // Z)))
                side = 1 if hop == CORE else 0
                label = ("g", batch, number, name)
                copies[label] = remote(
                    rows.at[batch, 0, xs, ys, zs, :, lanes],
                    rows.at[(batch, side) + landing + (slice(None), lanes)],
                    label,
                    hop,
                )
            label = ("r", batch, number, "c")
            copies[label] = remote(
                parts.at[batch, 1, :, :, :, :, lanes],
                arrived.at[batch, 1, :, :, :, :, lanes],
                label,
                CORE,
            )
            for _, sends, _ in reduce_steps(order):
                for name, hop, (xs, ys, zs) in sends:
                    label = ("r", batch, number, name)
                    copies[label] = remote(
                        parts.at[batch, 0, xs, ys, zs, :, lanes],
                        arrived.at[batch, 0, xs, ys, zs, :, lanes],
                        label,
                        hop,
                    )

    chosen = (lane_of == expert) | (lane_of == experts + expert)
    hidden_units = gate_w.shape[0]
    ups = lane_pieces(0, hidden_units, 256)
    rowwise = (((1,), (1,)), ((), ()))

    def up_piece(batch, side, piece):
        low, high = ups[piece]
        slab = rows[batch, side, :, :, :, :, :model_width].reshape(group * tokens, model_width)
        gate = lax.dot_general(
            slab, gate_w[low:high, :], rowwise, preferred_element_type=jnp.float32
        )
        upward = lax.dot_general(
            slab, up_w[low:high, :], rowwise, preferred_element_type=jnp.float32
        )
        act[side, :, low:high] = (
            (upward + 1.0) * gate * jax.nn.sigmoid(swish_scale * gate)
        ).astype(jnp.bfloat16)

    def down_piece(batch, number, side):
        low, high, _ = streams[number]
        ends = rows[batch, side, :, :, :, :, model_width:].reshape(group * tokens, tail)
        weight = jnp.sum(jnp.where(chosen, ends.astype(jnp.float32), 0.0), axis=1, keepdims=True)
        for start, stop in lane_pieces(low, min(high, model_width), 512):
            part = jnp.dot(
                act[side], down_w[:, start:stop], preferred_element_type=jnp.float32
            )
            parts[batch, side, :, :, :, :, start:stop] = (
                (part * weight).astype(parts.dtype).reshape(2, 2, PLANES, tokens, stop - start)
            )

    def reduce_piece(batch, number, index):
        low, high, order = streams[number]
        target, sends, others = reduce_steps(order)[index]
        stop = high if sends else min(high, model_width)
        held = rows_of(target)
        for place, (x, y, z) in enumerate(held):
            total = parts[batch, 0, x, y, z, :, low:stop].astype(jnp.float32)
            if not sends:
                total = total + hidden_ref[batch, :, low:stop].astype(jnp.float32)
            total = total + arrived[batch, 1, x, y, z, :, low:stop].astype(jnp.float32)
            for _, block_rows in others:
                inside = rows_of(block_rows)
                matching = inside if len(held) == 1 else [inside[place]]
                for ox, oy, oz in matching:
                    total = total + arrived[batch, 0, ox, oy, oz, :, low:stop].astype(jnp.float32)
            if sends:
                parts[batch, 0, x, y, z, :, low:stop] = total.astype(parts.dtype)
            else:
                out_ref[batch, :, low:stop] = total.astype(out_ref.dtype)

    parts[:, :, :, :, :, :, model_width:] = jnp.zeros(parts.shape[:-1] + (tail,), parts.dtype)
    landed, loaded = set(), set()
    actions = all_actions(micro_count, tokens, width, model_width, ups)
    for key, needs, _, sends in plan_actions(actions)[0]:
        for need in needs:
            if need in copies and need not in landed:
                landed.add(need)
                copies[need].wait_recv()
        kind, batch, number, index = key
        if kind == "u":
            if kind not in loaded:
                loads[0].wait()
                loads[1].wait()
            up_piece(batch, number, index)
        elif kind == "d":
            if kind not in loaded:
                loads[2].wait()
            down_piece(batch, number, index)
        elif kind == "a":
            reduce_piece(batch, number, index)
        loaded.add(kind)
        for label, _, _ in sends:
            copies[label].start()
    for label, copy in copies.items():
        if label not in landed:
            copy.wait_recv()
        copy.wait_send()


def tree_local(hidden, norm_gain, w_gate, w_up, w_down, expert_ids, route_weight):
    micro_count, tokens, model_width = hidden.shape
    devices = lax.axis_size("req")
    width = padded(model_width)
    hidden_units = w_gate.shape[1]
    vmem = pl.BlockSpec(memory_space=pltpu.VMEM)
    hbm = pl.BlockSpec(memory_space=pl.ANY)
    slots = (micro_count, 2, 2, 2, PLANES, tokens, width)
    messages = micro_count * sum(
        1 + len(gather_messages(order)) + sum(len(step[1]) for step in reduce_steps(order))
        for _, _, order in lane_streams(width)
    )
    return pl.pallas_call(
        tree_kernel,
        out_shape=jax.ShapeDtypeStruct(hidden.shape, hidden.dtype),
        in_specs=[vmem, vmem, vmem, vmem, hbm, hbm, hbm],
        out_specs=vmem,
        scratch_shapes=[
            pltpu.VMEM(slots, jnp.bfloat16),
            pltpu.VMEM(slots, jnp.bfloat16),
            pltpu.VMEM(slots, jnp.bfloat16),
            pltpu.VMEM((hidden_units, model_width), w_gate.dtype),
            pltpu.VMEM((hidden_units, model_width), w_up.dtype),
            pltpu.VMEM((hidden_units, model_width), w_down.dtype),
            pltpu.VMEM((2, devices // 2 * tokens, hidden_units), jnp.bfloat16),
            pltpu.SemaphoreType.DMA((3,)),
            pltpu.SemaphoreType.DMA((messages,)),
            pltpu.SemaphoreType.DMA((messages,)),
        ],
        compiler_params=pltpu.CompilerParams(
            collective_id=0, has_side_effects=True, vmem_limit_bytes=VMEM_BYTES
        ),
        name="tree",
    )(hidden, norm_gain[None, :], expert_ids, route_weight, w_gate.T, w_up.T, w_down)


def tree_fits(hidden, norm_gain, w_gate, w_up, w_down, expert_ids, route_weight):
    micro_count, tokens, model_width = hidden.shape
    devices = lax.axis_size("req")
    width = padded(model_width)
    units = w_gate.shape[1]
    slots = 3 * micro_count * devices * tokens * width
    weights = 3 * units * width
    work = 3 * devices * tokens * width
    return (
        devices == 8 * PLANES
        and 2 * (devices // HSPLIT) <= width - model_width
        and 2 * (slots + weights + work) <= VMEM_BYTES
    )


def local(*arguments):
    return (tree_local if tree_fits(*arguments) else routed_local)(*arguments)


def solution(mesh):
    return jax.shard_map(
        local,
        mesh=mesh,
        in_specs=(
            P(None, ("groups", "req"), None),
            P(),
            P(None, "req"),
            P(None, "req"),
            P("req", None),
            P(None, ("groups", "req"), None),
            P(None, ("groups", "req"), None),
        ),
        out_specs=P(None, ("groups", "req"), None),
        check_vma=False,
    )
```

time: 85.7 us -> 76.7 us (0.89)
  Pallas kernels: 79.4 us -> 70.8 us
  other arithmetic: 3.52 us -> 0 us
  local copies, waits for them, and re-layouts: 2.53 us -> 5.65 us
    pallas_call x1, Pallas kernels: 79.4 us -> 70.8 us  [tree_local(): pl.pallas_call(tree_kernel, out_shape=jax.ShapeDtypeStruct(hidden.shape,...]
    unnamed x1 -> x3, local copies, waits for them, and re-layouts: 1.61 us -> 4.35 us
    reduce_sum x2 -> x0, other arithmetic: 1.77 us -> none  [the longest x1 1.04 us: tree_local(): jnp.mean(residual * residual, axis=-1, keepdims=True) + epsilon]
    convert_element_type x3 -> x0, other arithmetic: 1.74 us -> none  [the longest x1 1.03 us: tree_local(): normed = (residual * lax.rsqrt(jnp.mean(residual * residual, axis=-1, kee...]
    broadcast_in_dim x1, local copies, waits for them, and re-layouts: 0.01 us -> 1.29 us  [tree_local(): norm_gain[None, :]]
where the time goes in v1:
time: 76.7 us; the launch traced here: 76.4 us
  Pallas kernels  70.8 us (92%)
  local copies, waits for them, and re-layouts  5.65 us (7%)
    pallas_call x1, Pallas kernels, tree_local(): pl.pallas_call(tree_kernel, out_shape=jax.ShapeDtypeStruct(hidden.shape,...  70.8 us
    unnamed x3, local copies, waits for them, and re-layouts  4.35 us

profile of v1, /device:TPU:0, one launch (start us, length us, event | category | flops | bytes accessed | tf_op | source)
XLA Modules:
  0.0 76.4 jit_solution(4888226667895706497)
XLA Ops:
  0.0 1.3 %broadcast_in_dim.3.gain_ref = bf16[1,2880]{1,0:T(2,128)(2,1)} reshape(bf16[2880]{0:T(1024)(128)(2,1)} %param.8) | data formatting | bytes 11520 | tf_op jit(solution)/shard_map/broadcast_in_dim | solution.py:546
  1.3 1.4 %copy.8.ids_ref = s32[2,16,4]{2,1,0:T(8,128)} copy(s32[2,16,4]{1,2,0:T(4,128)} %param.12) | data formatting | bytes 1024 | tf_op args[5]
  2.7 1.4 %copy.9.weight_ref = f32[2,16,4]{2,1,0:T(8,128)} copy(f32[2,16,4]{1,2,0:T(4,128)} %param.13) | data formatting | bytes 1024 | tf_op args[6]
  4.0 70.8 %tree.1 = bf16[2,16,2880]{2,1,0:T(8,128)(2,1)} custom-call(bf16[2,16,2880]{2,1,0:T(8,128)(2,1)} %hidden_ref.1, bf16[1,2880]{1,0:T(2,128)(2,1)} %broadcast_in_dim.3.gain_ref, s32[2,16,4]{2,1,0:T(8,128)} %copy.8.ids_ref, f32[2,16,4]{2,1,0:T(8,128)} %copy.9.weight_ref, bf16[720,2880]{1,0:T(8,128)(2,1)} %bitcast.2, bf16[720,2880]{1,0:T(8,128)(2,1)} %bitcast.3, ...), custom_call_target="tpu_custom_call" | custom-call | tf_op jit(solution)/shard_map/tree/pallas_call | solution.py:525
  74.8 1.6 %copy.11 = bf16[2,16,2880]{2,1,0:T(8,128)(2,1)} copy(bf16[2,16,2880]{2,1,0:T(8,128)(2,1)} %tree.1) | data formatting | bytes 368640

commit v2 on v1

--- a/solution.py
+++ b/solution.py
@@ -97,11 +97,34 @@
 LANES = 128
 PLANES = 4
 CORE, X, Y, Z = 1, 2, 4, 8
-SHARES = ((8, "zyx"), (10, "zxy"), (5, "yxz"))
+GROUPS = (
+    ((3, "zyx"), (3, "zxy")),
+    ((2, "yxz"), (3, "zxy"), (4, "zyx")),
+    ((4, "yxz"), (4, "zyx")),
+)
+PREFERENCE = {
+    ("s", 0): 0,
+    ("s", 1): 1,
+    ("a", 0): 0,
+    ("a", 1): 1,
+    ("u", 0): 3,
+    ("u", 1): 4,
+    ("d", 0): 2,
+    ("d", 1): 5,
+}
+SHARES = tuple(stream for members in GROUPS for stream in members)
+HELD = 1
 VMEM_BYTES = 60 * 1024 * 1024
-LINK_RATE, CORE_RATE = 47.5e3, 350e3
-CORE_DELAY, HOP_DELAY, FURTHER_DELAY = 1.0, 1.7, 0.8
-UP_SPAN, DOWN_SPAN, ADD_SPAN, STEP_SPAN = 0.9, 0.5, 0.01, 0.02
+LINK_RATE, CORE_RATE = 48.5e3, 570e3
+LINKS = {
+    CORE: (((CORE, 1),), 1.06),
+    X: (((X, 1),), 1.86),
+    Y: (((Y, 1),), 1.86),
+    Z: (((Z, 1),), 1.86),
+    2 * Z: (((Z, 1), (2 * Z, 2)), 2.66),
+    3 * Z: (((Z, 1), (2 * Z, 2)), 3.41),
+}
+UP_SPAN, DOWN_SPAN, ADD_SPAN, STEP_SPAN = 2.96, 0.7, 0.0116, 0.085
 ROW = slice(0, 1)
 PAIR = slice(0, 2)
 
@@ -141,10 +164,7 @@
             ("z2", 2 * Z, square, ("x0", "xy")),
             ("z1", Z, square, ("x0", "xy")),
             ("z3", Z, (PAIR, PAIR, one(2)), ("z2",)),
-            ("c0", CORE, square, ("x0", "xy")),
-            ("c2", CORE, (PAIR, PAIR, one(2)), ("z2",)),
-            ("c1", CORE, (PAIR, PAIR, one(1)), ("z1",)),
-            ("c3", CORE, (PAIR, PAIR, one(3)), ("z3",)),
+            ("c", CORE, (PAIR, PAIR, every), ("x0", "xy", "z1", "z2", "z3")),
         ]
         return messages
     far, near = (X, Y) if order == "zyx" else (Y, X)
@@ -157,11 +177,7 @@
         ("fz", far, (ROW, ROW, later), planes),
         ("fn", far, block(order, ROW, one(1), ROW), ("n0",)),
         ("fnz", far, block(order, ROW, one(1), later), ("nz",)),
-        ("c0", CORE, own, ()),
-        ("cz", CORE, (ROW, ROW, later), planes),
-        ("cn", CORE, block(order, ROW, one(1), every), ("n0", "nz")),
-        ("cf", CORE, block(order, one(1), ROW, every), ("f0", "fz")),
-        ("cfn", CORE, block(order, one(1), one(1), every), ("fn", "fnz")),
+        ("c", CORE, (PAIR, PAIR, every), ("f0", "fz", "fn", "fnz")),
     ]
     return messages
 
@@ -222,6 +238,18 @@
     ]
 
 
+def together(label, order):
+    kind, _, _, name = label
+    planes = ("z1", "z2", "z3")
+    if order != "yxz" and name in planes:
+        return planes, (ROW, ROW, slice(1, PLANES))
+    if kind == "g" and order == "yxz" and name in ("x0", "xy"):
+        return ("x0", "xy"), (one(1), PAIR, ROW)
+    if kind == "g" and order != "yxz" and name in ("f0", "fz", "fn", "fnz"):
+        return ("f0", "fz", "fn", "fnz"), block(order, one(1), PAIR, slice(0, PLANES))
+    return None
+
+
 def rows_of(rows):
     return [
         (x, y, z)
@@ -235,57 +263,76 @@
     return [(start, min(high, start + size)) for start in range(low, high, size)]
 
 
-def all_actions(micro_count, tokens, width, model_width, ups):
+def group_streams(group):
+    first = sum(len(members) for members in GROUPS[:group])
+    return range(first, first + len(GROUPS[group]))
+
+
+def all_actions(micro_count, tokens, width, ups):
     streams = lane_streams(width)
+    whole = 2 * PLANES * 4 * tokens
     actions = []
     for batch in range(micro_count):
         for number, (low, high, order) in enumerate(streams):
             for name, hop, rows, needs in gather_messages(order):
-                label = ("g", batch, number, name)
                 needed = [("g", batch, number, need) for need in needs]
                 if batch and not needs:
-                    needed = [("s", batch - 1, 0, "fz"), ("s", batch - 1, 1, "fz")]
-                size = 2 * len(rows_of(rows)) * tokens * (high - low)
-                actions.append((("s", batch, number, name), needed, STEP_SPAN, [(label, hop, size)]))
+                    needed = [("s", batch - 1, HELD, gather_messages(streams[HELD][2])[-2][0])]
+                made = [(("g", batch, number, name), hop, rows, low, high)]
+                actions.append((("s", batch, number, name), needed, STEP_SPAN, made))
     for batch in range(micro_count):
         for number, (low, high, order) in enumerate(streams):
+            group = [number in group_streams(index) for index in range(len(GROUPS))].index(True)
             for index, (rows, sends, arrived) in enumerate(reduce_steps(order)):
-                needed = [("d", batch, number, 0), ("r", batch, number, "c")]
+                needed = [("d", batch, group, 0), ("r", batch, number, "c")]
                 needed += [("r", batch, number, name) for name, _ in arrived]
-                count = len(rows_of(rows))
                 made = [
-                    (("r", batch, number, name), hop, 2 * len(rows_of(sent)) * tokens * (high - low))
-                    for name, hop, sent in sends
+                    (("r", batch, number, name), hop, sent, low, high) for name, hop, sent in sends
                 ]
-                span = STEP_SPAN + ADD_SPAN * count * (2 + len(arrived)) * (high - low) / 1024
+                count = len(rows_of(rows)) * (2 + len(arrived))
+                span = STEP_SPAN + ADD_SPAN * count * (high - low) / 1024
                 actions.append((("a", batch, number, index), needed, span, made))
+    every = (PAIR, PAIR, slice(0, PLANES))
     for batch in range(micro_count):
-        done = []
-        for side in (0, 1):
-            for piece in range(len(ups)):
+        before = [("d", batch - 1, group, side) for group in range(len(GROUPS)) for side in (0, 1)]
+        before = before if batch else []
+        for group in range(len(GROUPS)):
+            numbers = group_streams(group)
+            share = sum(streams[number][1] - streams[number][0] for number in numbers) / width
+            for side in (0, 1):
                 needed = [
                     ("g", batch, number, name)
-                    for number, (_, _, order) in enumerate(streams)
-                    for name, hop, _, _ in gather_messages(order)
+                    for number in numbers
+                    for name, hop, _, _ in gather_messages(streams[number][2])
                     if (hop == CORE) == bool(side)
                 ]
-                actions.append((("u", batch, side, piece), needed + done[-1:], UP_SPAN, []))
-                done.append(("u", batch, side, piece))
-        for number, (low, high, order) in enumerate(streams):
+                for piece in range(len(ups)):
+                    earlier = [("u", batch, group - 1, side, piece)] if group else before
+                    span = UP_SPAN * share / len(ups)
+                    actions.append((("u", batch, group, side, piece), needed + earlier, span, []))
+        done = [
+            ("u", batch, len(GROUPS) - 1, side, piece) for side in (0, 1) for piece in range(len(ups))
+        ]
+        for group in range(len(GROUPS)):
+            numbers = group_streams(group)
+            share = sum(streams[number][1] - streams[number][0] for number in numbers) / width
             for side in (1, 0):
-                made = []
-                if side:
-                    size = 2 * PLANES * 4 * tokens * (high - low)
-                    made = [(("r", batch, number, "c"), CORE, size)]
-                span = DOWN_SPAN * (high - low) / 1024
-                actions.append((("d", batch, number, side), done[-1:], span, made))
-                done.append(("d", batch, number, side))
+                made = [
+                    (("r", batch, number, "c"), CORE, every) + streams[number][:2]
+                    for number in numbers
+                    if side
+                ]
+                actions.append((("d", batch, group, side), done, DOWN_SPAN * share, made))
+                done = done + [("d", batch, group, side)]
     return actions
 
 
-def plan_actions(actions):
+def plan_actions(actions, tokens):
     moment, ready_at, link_free, order = 0.0, {}, {}, []
-    left = list(actions)
+    left = sorted(
+        actions,
+        key=lambda action: (PREFERENCE[action[0][:2]], {"s": 0, "a": 0}.get(action[0][0], 0) * action[0][2]),
+    )
     while left:
         best = None
         for action in left:
@@ -301,12 +348,13 @@
         order.append(action)
         moment = max(moment, start) + action[2]
         ready_at[action[0]] = moment
-        for label, hop, size in action[3]:
-            link = "z" if hop >= Z else hop
-            rate = CORE_RATE if hop == CORE else LINK_RATE
-            delay = CORE_DELAY if hop == CORE else HOP_DELAY + FURTHER_DELAY * (hop > Z)
-            link_free[link] = max(link_free.get(link, 0.0), moment) + size / rate
-            ready_at[label] = link_free[link] + delay
+        for label, hop, rows, low, high in action[3]:
+            span = 2 * len(rows_of(rows)) * tokens * (high - low)
+            span = span / (CORE_RATE if hop == CORE else LINK_RATE)
+            used, delay = LINKS[hop]
+            for link, times in used:
+                link_free[link] = max(link_free.get(link, 0.0), moment) + span * times
+            ready_at[label] = max(link_free[link] for link, _ in used) + delay
     return order, moment
 
 
@@ -326,14 +374,17 @@
     up_w,
     down_w,
     act,
+    gate_part,
+    up_part,
     weight_sems,
-    send_sems,
+    send_sem,
     recv_sems,
+    sent,
 ):
     micro_count, tokens, model_width = hidden_ref.shape
     width = rows.shape[-1]
     devices = lax.axis_size("req")
-    group = devices // 2
+    half = devices // 2
     me = lax.axis_index("req")
     experts = devices // HSPLIT
     expert = me // HSPLIT
@@ -365,19 +416,21 @@
 
     tail = width - model_width
     lane_of = lax.broadcasted_iota(jnp.int32, (1, tail), 1)
-    gain = gain_ref[...].astype(jnp.float32)
+    line_of = lax.broadcasted_iota(jnp.int32, (tail, 1), 0)
+    named = line_of - experts * (line_of // experts)
+    gain = gain_ref[...].astype(jnp.float32)[None, :]
     for batch in range(micro_count):
         residual = hidden_ref[batch].astype(jnp.float32)
         scale = lax.rsqrt(jnp.mean(residual * residual, axis=-1, keepdims=True) + epsilon)
         rows[batch, 0, 0, 0, 0, :, :model_width] = (residual * scale * gain).astype(jnp.bfloat16)
-        named = lane_of - experts * (lane_of // experts)
-        table = jnp.zeros((tokens, tail), jnp.float32)
-        for member in range(ids_ref.shape[2]):
+        table = jnp.zeros((tail, tokens), jnp.float32)
+        for member in range(ids_ref.shape[1]):
             table = table + jnp.where(
-                ids_ref[batch, :, member : member + 1] == named,
-                weight_ref[batch, :, member : member + 1],
+                ids_ref[batch, member : member + 1, :] == named,
+                weight_ref[batch, member : member + 1, :],
                 0.0,
             )
+        table = table.T
         upper = table.astype(jnp.bfloat16).astype(jnp.float32)
         shown = jnp.where(lane_of < experts, upper, table - upper)
         shown = jnp.where(lane_of < 2 * experts, shown, 0.0)
@@ -385,17 +438,29 @@
     pl.semaphore_wait(barrier, len(hops))
 
     slots = {}
+    waits = {}
 
     def remote(source, target, label, hop):
-        number = slots.setdefault(label, len(slots))
-        return pltpu.make_async_remote_copy(
+        kind, batch, number, name = label
+        low, high, order = streams[number]
+        taken = together(label, order)
+        key = label if taken is None else label[:3] + taken[0]
+        slot = slots.setdefault(key, len(slots))
+        copy = pltpu.make_async_remote_copy(
             src_ref=source,
             dst_ref=target,
-            send_sem=send_sems.at[number],
-            recv_sem=recv_sems.at[number],
+            send_sem=send_sem,
+            recv_sem=recv_sems.at[slot],
             device_id={"req": partner[hop]},
             device_id_type=pl.DeviceIdType.MESH,
         )
+        if taken is None:
+            waits[label] = (key, copy.wait_recv)
+        else:
+            xs, ys, zs = taken[1]
+            whole = (rows if kind == "g" else arrived).at[batch, 0, xs, ys, zs, :, low:high]
+            waits[label] = (key, pltpu.make_async_copy(whole, whole, recv_sems.at[slot]).wait)
+        return copy
 
     copies = {}
     for batch in range(micro_count):
@@ -436,24 +501,34 @@
     ups = lane_pieces(0, hidden_units, 256)
     rowwise = (((1,), (1,)), ((), ()))
 
-    def up_piece(batch, side, piece):
+    def up_piece(batch, group, side, piece):
         low, high = ups[piece]
-        slab = rows[batch, side, :, :, :, :, :model_width].reshape(group * tokens, model_width)
+        numbers = group_streams(group)
+        start, stop = streams[numbers[0]][0], min(streams[numbers[-1]][1], model_width)
+        slab = rows[batch, side, :, :, :, :, start:stop].reshape(half * tokens, stop - start)
         gate = lax.dot_general(
-            slab, gate_w[low:high, :], rowwise, preferred_element_type=jnp.float32
+            slab, gate_w[low:high, start:stop], rowwise, preferred_element_type=jnp.float32
         )
         upward = lax.dot_general(
-            slab, up_w[low:high, :], rowwise, preferred_element_type=jnp.float32
-        )
-        act[side, :, low:high] = (
-            (upward + 1.0) * gate * jax.nn.sigmoid(swish_scale * gate)
-        ).astype(jnp.bfloat16)
-
-    def down_piece(batch, number, side):
-        low, high, _ = streams[number]
-        ends = rows[batch, side, :, :, :, :, model_width:].reshape(group * tokens, tail)
+            slab, up_w[low:high, start:stop], rowwise, preferred_element_type=jnp.float32
+        )
+        if group:
+            gate = gate_part[side, :, low:high] + gate
+            upward = up_part[side, :, low:high] + upward
+        if group < len(GROUPS) - 1:
+            gate_part[side, :, low:high] = gate
+            up_part[side, :, low:high] = upward
+        else:
+            act[side, :, low:high] = (
+                (upward + 1.0) * gate * jax.nn.sigmoid(swish_scale * gate)
+            ).astype(jnp.bfloat16)
+
+    def down_piece(batch, group, side):
+        numbers = group_streams(group)
+        low, high = streams[numbers[0]][0], min(streams[numbers[-1]][1], model_width)
+        ends = rows[batch, side, :, :, :, :, model_width:].reshape(half * tokens, tail)
         weight = jnp.sum(jnp.where(chosen, ends.astype(jnp.float32), 0.0), axis=1, keepdims=True)
-        for start, stop in lane_pieces(low, min(high, model_width), 512):
+        for start, stop in lane_pieces(low, high, 512):
             part = jnp.dot(
                 act[side], down_w[:, start:stop], preferred_element_type=jnp.float32
             )
@@ -483,31 +558,28 @@
 
     parts[:, :, :, :, :, :, model_width:] = jnp.zeros(parts.shape[:-1] + (tail,), parts.dtype)
     landed, loaded = set(), set()
-    actions = all_actions(micro_count, tokens, width, model_width, ups)
-    for key, needs, _, sends in plan_actions(actions)[0]:
+    actions = all_actions(micro_count, tokens, width, ups)
+    for key, needs, _, sends in plan_actions(actions, tokens)[0]:
         for need in needs:
-            if need in copies and need not in landed:
-                landed.add(need)
-                copies[need].wait_recv()
-        kind, batch, number, index = key
+            if need in waits and waits[need][0] not in landed:
+                landed.add(waits[need][0])
+                waits[need][1]()
+        kind = key[0]
         if kind == "u":
             if kind not in loaded:
                 loads[0].wait()
                 loads[1].wait()
-            up_piece(batch, number, index)
+            up_piece(*key[1:])
         elif kind == "d":
             if kind not in loaded:
                 loads[2].wait()
-            down_piece(batch, number, index)
+            down_piece(*key[1:])
         elif kind == "a":
-            reduce_piece(batch, number, index)
+            reduce_piece(*key[1:])
         loaded.add(kind)
-        for label, _, _ in sends:
+        for label, *_ in sends:
             copies[label].start()
-    for label, copy in copies.items():
-        if label not in landed:
-            copy.wait_recv()
-        copy.wait_send()
+    pltpu.make_async_copy(sent, sent, send_sem).wait()
 
 
 def tree_local(hidden, norm_gain, w_gate, w_up, w_down, expert_ids, route_weight):
@@ -518,9 +590,23 @@
     vmem = pl.BlockSpec(memory_space=pltpu.VMEM)
     hbm = pl.BlockSpec(memory_space=pl.ANY)
     slots = (micro_count, 2, 2, 2, PLANES, tokens, width)
-    messages = micro_count * sum(
-        1 + len(gather_messages(order)) + sum(len(step[1]) for step in reduce_steps(order))
-        for _, _, order in lane_streams(width)
+    labels = [
+        (kind, batch, number, name)
+        for batch in range(micro_count)
+        for number, (_, _, order) in enumerate(lane_streams(width))
+        for kind, names in (
+            ("g", [message[0] for message in gather_messages(order)]),
+            ("r", ["c"] + [name for step in reduce_steps(order) for name, _, _ in step[1]]),
+        )
+        for name in names
+    ]
+    orders = [order for _, _, order in lane_streams(width)]
+    grouped = [together(label, orders[label[2]]) for label in labels]
+    messages = len(
+        {
+            label if taken is None else label[:3] + taken[0]
+            for label, taken in zip(labels, grouped)
+        }
     )
     return pl.pallas_call(
         tree_kernel,
@@ -535,15 +621,26 @@
             pltpu.VMEM((hidden_units, model_width), w_up.dtype),
             pltpu.VMEM((hidden_units, model_width), w_down.dtype),
             pltpu.VMEM((2, devices // 2 * tokens, hidden_units), jnp.bfloat16),
+            pltpu.VMEM((2, devices // 2 * tokens, hidden_units), jnp.float32),
+            pltpu.VMEM((2, devices // 2 * tokens, hidden_units), jnp.float32),
             pltpu.SemaphoreType.DMA((3,)),
+            pltpu.SemaphoreType.DMA,
             pltpu.SemaphoreType.DMA((messages,)),
-            pltpu.SemaphoreType.DMA((messages,)),
+            pltpu.VMEM((2 * micro_count * (devices - 1), tokens, width), jnp.bfloat16),
         ],
         compiler_params=pltpu.CompilerParams(
             collective_id=0, has_side_effects=True, vmem_limit_bytes=VMEM_BYTES
         ),
         name="tree",
-    )(hidden, norm_gain[None, :], expert_ids, route_weight, w_gate.T, w_up.T, w_down)
+    )(
+        hidden,
+        norm_gain,
+        expert_ids.transpose(0, 2, 1),
+        route_weight.transpose(0, 2, 1),
+        w_gate.T,
+        w_up.T,
+        w_down,
+    )
 
 
 def tree_fits(hidden, norm_gain, w_gate, w_up, w_down, expert_ids, route_weight):

time: 76.7 us -> 68.1 us (0.89)
  Pallas kernels: 70.8 us -> 66.3 us
  local copies, waits for them, and re-layouts: 5.65 us -> 1.61 us
    pallas_call x1, Pallas kernels: 70.8 us -> 66.3 us  [tree_local(): pl.pallas_call(tree_kernel, out_shape=jax.ShapeDtypeStruct(hidden.shape,...]
    unnamed x3 -> x1, local copies, waits for them, and re-layouts: 4.35 us -> 1.61 us
    broadcast_in_dim x1 -> x0, local copies, waits for them, and re-layouts: 1.29 us -> none  [tree_local(): norm_gain[None, :]]
where the time goes in v2:
time: 68.1 us; the launch traced here: 67.9 us
  Pallas kernels  66.3 us (97%)
  local copies, waits for them, and re-layouts  1.61 us (2%)
    pallas_call x1, Pallas kernels, tree_local(): pl.pallas_call(tree_kernel, out_shape=jax.ShapeDtypeStruct(hidden.shape,...  66.3 us
    unnamed x1, local copies, waits for them, and re-layouts  1.61 us

profile of v2, /device:TPU:0, one launch (start us, length us, event | category | flops | bytes accessed | tf_op | source)
XLA Modules:
  0.0 67.9 jit_solution(14664032551707052847)
XLA Ops:
  0.0 66.3 %tree.1 = bf16[2,16,2880]{2,1,0:T(8,128)(2,1)} custom-call(bf16[2,16,2880]{2,1,0:T(8,128)(2,1)} %hidden_ref.1, bf16[2880]{0:T(1024)(128)(2,1)} %gain_ref.1, s32[2,4,16]{2,1,0:T(4,128)} %bitcast.6, f32[2,4,16]{2,1,0:T(4,128)} %bitcast.7, bf16[720,2880]{1,0:T(8,128)(2,1)} %bitcast.4, bf16[720,2880]{1,0:T(8,128)(2,1)} %bitcast.5, bf16[720,2880]{1,0:T(8,128)(2,1)} %down_hbm.1), custom_call_target="tpu_custom_call" | custom-call | tf_op jit(solution)/shard_map/tree/pallas_call | solution.py:611
  66.3 1.6 %copy.9 = bf16[2,16,2880]{2,1,0:T(8,128)(2,1)} copy(bf16[2,16,2880]{2,1,0:T(8,128)(2,1)} %tree.1) | data formatting | bytes 368640

commit v3 on v2

--- a/solution.py
+++ b/solution.py
@@ -98,33 +98,34 @@
 PLANES = 4
 CORE, X, Y, Z = 1, 2, 4, 8
 GROUPS = (
-    ((3, "zyx"), (3, "zxy")),
-    ((2, "yxz"), (3, "zxy"), (4, "zyx")),
-    ((4, "yxz"), (4, "zyx")),
+    ((6, "zxy"), (4, "zyx")),
+    ((5, "yxz"), (3, "zyx")),
+    ((5, "zxy"),),
 )
 PREFERENCE = {
     ("s", 0): 0,
-    ("s", 1): 1,
+    ("s", 1): 2,
     ("a", 0): 0,
     ("a", 1): 1,
-    ("u", 0): 3,
-    ("u", 1): 4,
-    ("d", 0): 2,
-    ("d", 1): 5,
+    ("u", 0): 4,
+    ("u", 1): 5,
+    ("d", 0): 3,
+    ("d", 1): 6,
 }
 SHARES = tuple(stream for members in GROUPS for stream in members)
-HELD = 1
+HELD = 3
 VMEM_BYTES = 60 * 1024 * 1024
-LINK_RATE, CORE_RATE = 48.5e3, 570e3
+LINK_RATE, CORE_RATE = 49.5e3, 1400e3
 LINKS = {
-    CORE: (((CORE, 1),), 1.06),
-    X: (((X, 1),), 1.86),
-    Y: (((Y, 1),), 1.86),
-    Z: (((Z, 1),), 1.86),
-    2 * Z: (((Z, 1), (2 * Z, 2)), 2.66),
-    3 * Z: (((Z, 1), (2 * Z, 2)), 3.41),
+    CORE: (((CORE, 1),), 1.12),
+    X: (((X, 1),), 1.92),
+    Y: (((Y, 1),), 1.92),
+    Z: (((Z, 1),), 1.92),
+    2 * Z: (((Z, 1), (2 * Z, 2)), 2.72),
+    3 * Z: (((Z, 1), (2 * Z, 2)), 3.47),
 }
-UP_SPAN, DOWN_SPAN, ADD_SPAN, STEP_SPAN = 2.96, 0.7, 0.0116, 0.085
+UP_SPAN, DOWN_SPAN, DOWN_START, ADD_SPAN = 2.58, 1.33, 0.08, 0.0144
+STEP_SPAN, SEND_SPAN, MESSAGE_SPAN = 0.092, 0.023, 0.034
 ROW = slice(0, 1)
 PAIR = slice(0, 2)
 
@@ -322,7 +323,7 @@
                     for number in numbers
                     if side
                 ]
-                actions.append((("d", batch, group, side), done, DOWN_SPAN * share, made))
+                actions.append((("d", batch, group, side), done, DOWN_START + DOWN_SPAN * share, made))
                 done = done + [("d", batch, group, side)]
     return actions
 
@@ -331,7 +332,7 @@
     moment, ready_at, link_free, order = 0.0, {}, {}, []
     left = sorted(
         actions,
-        key=lambda action: (PREFERENCE[action[0][:2]], {"s": 0, "a": 0}.get(action[0][0], 0) * action[0][2]),
+        key=lambda action: (PREFERENCE[action[0][:2]], {"s": 1, "a": 0}.get(action[0][0], 0) * action[0][2]),
     )
     while left:
         best = None
@@ -346,11 +347,11 @@
         start, action = best
         left.remove(action)
         order.append(action)
-        moment = max(moment, start) + action[2]
+        moment = max(moment, start) + action[2] + SEND_SPAN * len(action[3])
         ready_at[action[0]] = moment
         for label, hop, rows, low, high in action[3]:
             span = 2 * len(rows_of(rows)) * tokens * (high - low)
-            span = span / (CORE_RATE if hop == CORE else LINK_RATE)
+            span = span / (CORE_RATE if hop == CORE else LINK_RATE) + MESSAGE_SPAN
             used, delay = LINKS[hop]
             for link, times in used:
                 link_free[link] = max(link_free.get(link, 0.0), moment) + span * times
@@ -519,21 +520,23 @@
             gate_part[side, :, low:high] = gate
             up_part[side, :, low:high] = upward
         else:
+            ends = rows[batch, side, :, :, :, :, model_width:].reshape(half * tokens, tail)
+            weight = jnp.sum(
+                jnp.where(chosen, ends.astype(jnp.float32), 0.0), axis=1, keepdims=True
+            )
             act[side, :, low:high] = (
-                (upward + 1.0) * gate * jax.nn.sigmoid(swish_scale * gate)
+                weight * ((upward + 1.0) * gate * jax.nn.sigmoid(swish_scale * gate))
             ).astype(jnp.bfloat16)
 
     def down_piece(batch, group, side):
         numbers = group_streams(group)
         low, high = streams[numbers[0]][0], min(streams[numbers[-1]][1], model_width)
-        ends = rows[batch, side, :, :, :, :, model_width:].reshape(half * tokens, tail)
-        weight = jnp.sum(jnp.where(chosen, ends.astype(jnp.float32), 0.0), axis=1, keepdims=True)
         for start, stop in lane_pieces(low, high, 512):
             part = jnp.dot(
                 act[side], down_w[:, start:stop], preferred_element_type=jnp.float32
             )
             parts[batch, side, :, :, :, :, start:stop] = (
-                (part * weight).astype(parts.dtype).reshape(2, 2, PLANES, tokens, stop - start)
+                part.astype(parts.dtype).reshape(2, 2, PLANES, tokens, stop - start)
             )
 
     def reduce_piece(batch, number, index):

time: 68.1 us -> 66.6 us (0.978)
  Pallas kernels: 66.3 us -> 64.9 us
    pallas_call x1, Pallas kernels: 66.3 us -> 64.9 us  [tree_local(): pl.pallas_call(tree_kernel, out_shape=jax.ShapeDtypeStruct(hidden.shape,...]
where the time goes in v3:
time: 66.6 us; the launch traced here: 66.5 us
  Pallas kernels  64.9 us (97%)
  local copies, waits for them, and re-layouts  1.61 us (2%)
    pallas_call x1, Pallas kernels, tree_local(): pl.pallas_call(tree_kernel, out_shape=jax.ShapeDtypeStruct(hidden.shape,...  64.9 us
    unnamed x1, local copies, waits for them, and re-layouts  1.61 us

profile of v3, /device:TPU:0, one launch (start us, length us, event | category | flops | bytes accessed | tf_op | source)
XLA Modules:
  0.0 66.5 jit_solution(9701476735347963936)
XLA Ops:
  0.0 64.9 %tree.1 = bf16[2,16,2880]{2,1,0:T(8,128)(2,1)} custom-call(bf16[2,16,2880]{2,1,0:T(8,128)(2,1)} %hidden_ref.1, bf16[2880]{0:T(1024)(128)(2,1)} %gain_ref.1, s32[2,4,16]{2,1,0:T(4,128)} %bitcast.6, f32[2,4,16]{2,1,0:T(4,128)} %bitcast.7, bf16[720,2880]{1,0:T(8,128)(2,1)} %bitcast.4, bf16[720,2880]{1,0:T(8,128)(2,1)} %bitcast.5, bf16[720,2880]{1,0:T(8,128)(2,1)} %down_hbm.1), custom_call_target="tpu_custom_call" | custom-call | tf_op jit(solution)/shard_map/tree/pallas_call | solution.py:614
  64.9 1.6 %copy.9 = bf16[2,16,2880]{2,1,0:T(8,128)(2,1)} copy(bf16[2,16,2880]{2,1,0:T(8,128)(2,1)} %tree.1) | data formatting | bytes 368640

commit v4 on v3

--- a/solution.py
+++ b/solution.py
@@ -377,6 +377,7 @@
     act,
     gate_part,
     up_part,
+    scale_part,
     weight_sems,
     send_sem,
     recv_sems,
@@ -501,6 +502,7 @@
     hidden_units = gate_w.shape[0]
     ups = lane_pieces(0, hidden_units, 256)
     rowwise = (((1,), (1,)), ((), ()))
+    scaled = set()
 
     def up_piece(batch, group, side, piece):
         low, high = ups[piece]
@@ -520,10 +522,15 @@
             gate_part[side, :, low:high] = gate
             up_part[side, :, low:high] = upward
         else:
-            ends = rows[batch, side, :, :, :, :, model_width:].reshape(half * tokens, tail)
-            weight = jnp.sum(
-                jnp.where(chosen, ends.astype(jnp.float32), 0.0), axis=1, keepdims=True
-            )
+            if (batch, side) not in scaled:
+                scaled.add((batch, side))
+                ends = rows[batch, side, :, :, :, :, model_width:].reshape(half * tokens, tail)
+                total = jnp.sum(
+                    jnp.where(chosen, ends.astype(jnp.float32), 0.0), axis=1, keepdims=True
+                )
+                scale_part[side] = jnp.broadcast_to(total, scale_part.shape[1:])
+            copies_wide = -(-(high - low) // LANES)
+            weight = jnp.concatenate([scale_part[side]] * copies_wide, axis=1)[:, : high - low]
             act[side, :, low:high] = (
                 weight * ((upward + 1.0) * gate * jax.nn.sigmoid(swish_scale * gate))
             ).astype(jnp.bfloat16)
@@ -626,6 +633,7 @@
             pltpu.VMEM((2, devices // 2 * tokens, hidden_units), jnp.bfloat16),
             pltpu.VMEM((2, devices // 2 * tokens, hidden_units), jnp.float32),
             pltpu.VMEM((2, devices // 2 * tokens, hidden_units), jnp.float32),
+            pltpu.VMEM((2, devices // 2 * tokens, LANES), jnp.float32),
             pltpu.SemaphoreType.DMA((3,)),
             pltpu.SemaphoreType.DMA,
             pltpu.SemaphoreType.DMA((messages,)),

time: 66.6 us -> 67.4 us (1.012)
  Pallas kernels: 64.9 us -> 65.6 us
    pallas_call x1, Pallas kernels: 64.9 us -> 65.6 us  [tree_local(): pl.pallas_call(tree_kernel, out_shape=jax.ShapeDtypeStruct(hidden.shape,...]
where the time goes in v4:
time: 67.4 us; the launch traced here: 67.2 us
  Pallas kernels  65.6 us (97%)
  local copies, waits for them, and re-layouts  1.61 us (2%)
    pallas_call x1, Pallas kernels, tree_local(): pl.pallas_call(tree_kernel, out_shape=jax.ShapeDtypeStruct(hidden.shape,...  65.6 us
    unnamed x1, local copies, waits for them, and re-layouts  1.61 us

profile of v4, /device:TPU:0, one launch (start us, length us, event | category | flops | bytes accessed | tf_op | source)
XLA Modules:
  0.0 67.2 jit_solution(11988116341842510852)
XLA Ops:
  0.0 65.6 %tree.1 = bf16[2,16,2880]{2,1,0:T(8,128)(2,1)} custom-call(bf16[2,16,2880]{2,1,0:T(8,128)(2,1)} %hidden_ref.1, bf16[2880]{0:T(1024)(128)(2,1)} %gain_ref.1, s32[2,4,16]{2,1,0:T(4,128)} %bitcast.6, f32[2,4,16]{2,1,0:T(4,128)} %bitcast.7, bf16[720,2880]{1,0:T(8,128)(2,1)} %bitcast.4, bf16[720,2880]{1,0:T(8,128)(2,1)} %bitcast.5, bf16[720,2880]{1,0:T(8,128)(2,1)} %down_hbm.1), custom_call_target="tpu_custom_call" | custom-call | tf_op jit(solution)/shard_map/tree/pallas_call | solution.py:621
  65.6 1.6 %copy.9 = bf16[2,16,2880]{2,1,0:T(8,128)(2,1)} copy(bf16[2,16,2880]{2,1,0:T(8,128)(2,1)} %tree.1) | data formatting | bytes 368640
